TPU v7x, 256 devices: a whole 4x4x8 slice. The times are simulated.
256 devices in a mesh: dp: 4 (over x), space: 64 (over y, z, core).
Axes of the slice: x: 4, y: 4, z: 8, core: 2. Of those that a mesh axis runs over, the one named last changes fastest.
Arguments:
- volume: bfloat16 [4, 128, 128, 16, 256], P('dp', None, 'space'), may hold values from -6 to 6
- w_first: bfloat16 [3, 3, 3, 128, 256], replicated, may hold values from -0.109375 to 0.109375
- w_second: bfloat16 [3, 3, 3, 256, 512], P(None, None, None, 'space'), may hold values from -0.078125 to 0.078125
- cotangent: bfloat16 [4, 512, 32, 256], P('dp', 'space'), may hold values from -6 to 6
Outputs:
- grad_second: float32 [3, 3, 3, 256, 512], P(None, None, None, 'space')
- pre_grad: bfloat16 [4, 256, 64, 4, 256], P('dp', None, 'space')
All inputs are finite; a program needn't handle non-finite values.
Results may differ from a plain program's by a relative error of at most 0.0049.
Values may be sent and summed in bfloat16 or wider, within the bound.
No kernel may reach another device: no remote copies, remote signals or barrier semaphores. Data moves between devices by JAX's collectives and lax.ppermute only.
A program may use at most 128 MiB of HBM per device.

v0:
```python
import jax
import jax.numpy as jnp
from jax import lax
from jax.sharding import PartitionSpec as P

C3 = 512
WID = 128
leak_slope = 0.3


def from_behind(block, axis, distance):
    devices = range(lax.axis_size(axis))
    route = [(i - distance, i) for i in devices if i - distance in devices]
    return lax.ppermute(block, axis, route)


def activate(values):
    return leak_slope * values + (1.0 - leak_slope) * values * jax.nn.sigmoid(values)


def slope_of(values):
    sigmoid_value = jax.nn.sigmoid(values)
    return leak_slope + (1.0 - leak_slope) * (
        sigmoid_value + values * sigmoid_value * (1.0 - sigmoid_value)
    )


def stride_taps(values, along_dim):
    length = values.shape[along_dim] // 2
    paired = values.reshape(values.shape[:along_dim] + (length, 2) + values.shape[along_dim + 1 :])
    even_cells = lax.index_in_dim(paired, 0, along_dim + 1, keepdims=False)
    odd_cells = lax.index_in_dim(paired, 1, along_dim + 1, keepdims=False)
    before = jnp.concatenate(
        [
            jnp.zeros_like(lax.slice_in_dim(odd_cells, 0, 1, axis=along_dim)),
            lax.slice_in_dim(odd_cells, 0, length - 1, axis=along_dim),
        ],
        along_dim,
    )
    return [before, even_cells, odd_cells]


def step_cells(values, by_row, by_col, row_len):
    cells = values.shape[-1]
    if by_row:
        filler = jnp.zeros(values.shape[:-1] + (row_len,), values.dtype)
        values = jnp.concatenate([filler, values[..., : cells - row_len]], -1)
    if by_col:
        filler = jnp.zeros(values.shape[:-1] + (1,), values.dtype)
        moved = jnp.concatenate([filler, values[..., : cells - 1]], -1)
        keeper = lax.iota(jnp.int32, cells) % row_len != 0
        values = jnp.where(keeper, moved, jnp.zeros_like(moved))
    return values


def plane_taps(values, row_len):
    phases = values.shape[-2]
    out_phases = phases // 2
    collected = []
    for row_tap in range(3):
        for col_tap in range(3):
            rows_out = []
            for row_phase in range(out_phases):
                cols_out = []
                for col_phase in range(out_phases):
                    row_at = 2 * row_phase + row_tap - 1
                    col_at = 2 * col_phase + col_tap - 1
                    part = values[..., row_at % phases, col_at % phases, :]
                    cols_out.append(step_cells(part, row_at < 0, col_at < 0, row_len))
                rows_out.append(jnp.stack(cols_out, -2))
            collected.append(jnp.stack(rows_out, -3))
    return collected


def all_taps(values, row_len):
    collected = []
    for depth_part in stride_taps(values, 1):
        collected.extend(plane_taps(depth_part, row_len))
    return collected


def contract_first(left_side, right_side):
    return lax.dot_general(
        left_side, right_side, (((0,), (0,)), ((), ())), preferred_element_type=jnp.float32
    )


def contract_last(left_side, right_side):
    return lax.dot_general(
        left_side, right_side, (((1,), (1,)), ((), ())), preferred_element_type=jnp.float32
    )


def per_device(volume, w_first, w_second, cotangent):
    channels = volume.shape[1]
    depth_cells = volume.shape[2]
    cell_count = volume.shape[4]
    half_depth = depth_cells // 2
    out_channels = w_first.shape[4]
    row_len = WID // 4
    paired = volume[0].reshape(channels, half_depth, 2, 4, 4, cell_count)
    even_cells = paired[:, :, 0]
    odd_cells = paired[:, :, 1]
    w_flat = w_first.reshape(27 * channels, out_channels)
    rim_cells = from_behind(odd_cells, "space", 1)
    before = jnp.concatenate([rim_cells, odd_cells[:, : half_depth - 1]], 1)
    collected = []
    for depth_part in (before, even_cells, odd_cells):
        collected.extend(plane_taps(depth_part, row_len))
    stacked = jnp.stack(collected, 0).reshape(27 * channels, -1)
    pre_act = contract_first(w_flat, stacked).reshape(out_channels, half_depth, 4, cell_count)
    hidden = activate(pre_act).astype(jnp.bfloat16)
    by_channel = lax.all_to_all(hidden, "space", split_axis=0, concat_axis=1, tiled=True)
    own_channels = by_channel.shape[0]
    full_depth = by_channel.shape[1]
    hidden_cells = by_channel.reshape(own_channels, full_depth, 2, 2, cell_count)
    hidden_taps = jnp.stack(all_taps(hidden_cells, row_len), 0).reshape(27 * own_channels, -1)
    w_rows = w_second.reshape(27 * own_channels, C3)
    out_cells = hidden_taps.shape[1]
    gathered = lax.all_gather(cotangent[0], "space", axis=0, tiled=True)
    cot_flat = gathered.reshape(C3, out_cells)
    weight_grad = contract_last(hidden_taps, cot_flat)
    tap_terms = jnp.dot(w_rows, cot_flat, preferred_element_type=jnp.float32)
    grad_second = lax.psum(weight_grad, "dp").reshape(3, 3, 3, own_channels, C3)

    def spread(field):
        return jnp.stack(all_taps(field, row_len), 0).reshape(27 * own_channels, -1)

    unused, pull = jax.vjp(
        spread, jnp.zeros((own_channels, full_depth, 2, 2, cell_count), jnp.float32)
    )
    back_terms = pull(tap_terms)[0]
    back_terms = back_terms.astype(jnp.bfloat16).reshape(own_channels, full_depth, 4, cell_count)
    hidden_grad = lax.all_to_all(back_terms, "space", split_axis=1, concat_axis=0, tiled=True)
    pre_grad = (hidden_grad.astype(jnp.float32) * slope_of(pre_act)).astype(jnp.bfloat16)
    return (grad_second, pre_grad[None])


def solution(mesh):
    in_specs = (
        P("dp", None, "space", None, None),
        P(),
        P(None, None, None, "space", None),
        P("dp", "space", None, None),
    )
    out_specs = (P(None, None, None, "space", None), P("dp", None, "space", None, None))
    return jax.shard_map(
        per_device, mesh=mesh, in_specs=in_specs, out_specs=out_specs, check_vma=False
    )
```

profile of v0, /device:TPU:8, one launch (start us, length us, event | category | flops | bytes accessed | tf_op | source)
XLA Modules:
  0.0 217.8 jit_solution(14263887980538199394)
XLA Ops:
  7.2 0.7 all-gather.3.cloned.1.call-update
  7.9 2.8 %copy.103 = bf16[1,128,2,16,256]{4,1,3,2,0:T(8,128)(2,1)S(1)} copy(bf16[1,128,2,16,256]{4,3,2,1,0:T(8,128)(2,1)} %param.4) | data formatting | bytes 4194304 | tf_op args[0]
  10.9 1.9 collective-permute-start
  14.1 16.5 %collective-permute-done = bf16[128,1,4,4,256]{4,0,3,2,1:T(8,128)(2,1)S(1)} collective-permute-done((bf16[128,1,4,4,256]{4,0,3,2,1:T(8,128)(2,1)S(1)}, bf16[128,1,4,4,256]{4,0,3,2,1:T(8,128)(2,1)S(1)}, u32[]{:S(2)}, u32[]{:S(2)}) %collective-permute-start) | collective-permute-done | bytes 1048608 | tf_op jit(solution)/shard_map/ppermute | solution.py:14
  32.8 6.8 %copy.104 = bf16[27,128,1,2,2,256]{5,4,3,1,0,2:T(2,128)(2,1)} copy(bf16[27,128,1,2,2,256]{5,1,4,3,2,0:T(8,128)(2,1)S(1)} %fusion.33) | data formatting | bytes 14155776 | tf_op jit(solution)/shard_map/stack | solution.py:110
  39.6 16.2 %reshape.233 = bf16[3456,1024]{1,0:T(8,128)(2,1)} reshape(bf16[27,128,1,2,2,256]{5,4,3,1,0,2:T(2,128)(2,1)} %copy.104) | data formatting | bytes 14155776 | tf_op jit(solution)/shard_map/reshape | solution.py:110
  55.8 6.2 %fusion.2 = (bf16[256,1024]{0,1:T(8,128)(2,1)S(1)}, f32[1024,256]{1,0:T(8,128)}) fusion(bf16[3456,1024]{1,0:T(8,128)(2,1)} %reshape.233, bf16[3456,256]{1,0:T(8,128)(2,1)S(1)} %bitcast.641), kind=kOutput, calls=%fused_computation.9 | convolution fusion | flops 1814036480 | bytes 10420224 | tf_op jit(solution)/shard_map/dot_general | solution.py:83
  62.0 1.1 copy.105
  63.0 10.7 %all-to-all-start = ((bf16[256,1,4,256]{3,2,1,0:T(4,128)(2,1)}), bf16[256,1,4,256]{3,2,1,0:T(4,128)(2,1)S(1)}, u32[]{:S(2)}, u32[]{:S(2)}) async-start(bf16[256,1,4,256]{3,2,1,0:T(4,128)(2,1)} %copy.105), calls=%async_computation | async-start | bytes 1048576 | tf_op jit(solution)/shard_map/all_to_all | solution.py:113
  73.9 1.6 copy.142
  75.5 20.0 %all-to-all-done = bf16[256,1,4,256]{3,2,1,0:T(4,128)(2,1)S(1)} async-done(((bf16[256,1,4,256]{3,2,1,0:T(4,128)(2,1)}), bf16[256,1,4,256]{3,2,1,0:T(4,128)(2,1)S(1)}, u32[]{:S(2)}, u32[]{:S(2)}) %all-to-all-start) | async-done | bytes 524320 | tf_op jit(solution)/shard_map/all_to_all | solution.py:113
  96.4 0.7 constant_dynamic-update-slice_fusion.26
  97.1 0.7 constant_dynamic-update-slice_fusion.25
  97.8 0.7 constant_dynamic-update-slice_fusion.24
  98.5 0.7 constant_dynamic-update-slice_fusion.23
  99.3 0.7 constant_dynamic-update-slice_fusion.22
  99.9 0.6 constant_dynamic-update-slice_fusion.21
  100.6 0.7 constant_dynamic-update-slice_fusion.20
  101.3 0.7 constant_dynamic-update-slice_fusion.19
  102.0 0.7 constant_dynamic-update-slice_fusion.18
  102.8 0.7 constant_dynamic-update-slice_fusion.17
  103.6 0.7 constant_dynamic-update-slice_fusion.16
  104.3 0.7 constant_dynamic-update-slice_fusion.15
  105.2 0.7 constant_dynamic-update-slice_fusion.14
  105.9 0.7 constant_dynamic-update-slice_fusion.13
  106.6 0.6 constant_dynamic-update-slice_fusion.12
  107.2 0.7 constant_dynamic-update-slice_fusion.11
  108.0 0.7 constant_dynamic-update-slice_fusion.10
  109.3 0.7 constant_dynamic-update-slice_fusion.8
  110.0 0.7 constant_dynamic-update-slice_fusion.7
  110.7 0.7 constant_dynamic-update-slice_fusion.6
  111.5 0.7 constant_dynamic-update-slice_fusion.5
  112.2 0.6 constant_dynamic-update-slice_fusion.4
  113.5 0.7 constant_dynamic-update-slice_fusion.2
  114.3 16.7 %copy.149 = bf16[64,8,32,256]{3,1,2,0:T(8,128)(2,1)} copy(bf16[64,8,32,256]{3,2,1,0:T(8,128)(2,1)} %bitcast.644) | data formatting | bytes 16777216
  131.0 4.7 %fusion.42 = f32[108,8192]{1,0:T(8,128)S(1)} fusion(bf16[108,512]{1,0:T(8,128)(2,1)S(1)} %reshape.238, bf16[512,8192]{1,0:T(8,128)(2,1)} %bitcast.642), kind=kOutput, calls=%fused_computation.302 | convolution fusion | flops 905969664 | bytes 12038144 | tf_op jit(solution)/shard_map/dot_general | solution.py:123
  136.3 0.7 slice_select_fusion.8
  139.5 1.1 copy.140
  140.6 7.1 %all-to-all-start.1 = ((bf16[4,64,4,256]{3,0,2,1:T(4,128)(2,1)}), bf16[4,64,4,256]{3,0,2,1:T(4,128)(2,1)S(1)}, u32[]{:S(2)}, u32[]{:S(2)}) async-start(bf16[4,64,4,256]{3,0,2,1:T(4,128)(2,1)} %bitcast.260), calls=%async_computation.1 | async-start | bytes 1048576 | tf_op jit(solution)/shard_map/all_to_all | solution.py:134
  148.6 0.6 constant_dynamic-update-slice_fusion
  149.3 1.8 copy.111
  151.3 1.2 copy.150
  152.5 7.1 %fusion.41 = f32[108,512]{1,0:T(8,128)} fusion(bf16[108,8192]{1,0:T(8,128)(2,1)S(1)} %bitcast.646, bf16[512,8192]{1,0:T(8,128)(2,1)} %bitcast.643), kind=kOutput, calls=%fused_computation.301 | convolution fusion | flops 905969664 | bytes 10379264 | tf_op jit(solution)/shard_map/dot_general | solution.py:89
  159.7 1.7 reshape.237
  161.4 3.0 %all-to-all-done.1 = bf16[4,64,4,256]{3,0,2,1:T(4,128)(2,1)S(1)} async-done(((bf16[4,64,4,256]{3,0,2,1:T(4,128)(2,1)}), bf16[4,64,4,256]{3,0,2,1:T(4,128)(2,1)S(1)}, u32[]{:S(2)}, u32[]{:S(2)}) %all-to-all-start.1) | async-done | bytes 524320 | tf_op jit(solution)/shard_map/all_to_all | solution.py:134
  164.9 1.8 fusion
  166.7 42.7 %all-reduce.93.cloned.1.call-done = f32[3,3,3,4,512]{4,3,2,1,0:T(4,128)} async-done(((f32[3,3,3,4,512]{4,3,2,1,0:T(4,128)}), f32[3,3,3,4,512]{4,3,2,1,0:T(4,128)}) %all-reduce.93.cloned.1.call-update) | async-done | bytes 221200 | tf_op jit(solution)/shard_map/psum | solution.py:124
  209.4 1.6 copy.206
  (122 shorter events, 10.4 us)
Async XLA Ops:
  7.2 48.6 %copy-start = (bf16[3,3,3,128,256]{4,3,2,1,0:T(8,128)(2,1)S(1)}, bf16[3,3,3,128,256]{4,3,2,1,0:T(8,128)(2,1)}, u32[]{:S(2)}) copy-start(bf16[3,3,3,128,256]{4,3,2,1,0:T(8,128)(2,1)} %param.5) | copy-start | bytes 5308420
  7.2 107.1 %all-gather.3.cloned.1.call-start = ((), (), s32[]{:S(2)}) async-start(), calls=%async_computation.3 | async-start | bytes 8519680 | tf_op jit(solution)/shard_map/all_gather | solution.py:120
  10.9 19.7 %collective-permute-start = (bf16[128,1,4,4,256]{4,0,3,2,1:T(8,128)(2,1)S(1)}, bf16[128,1,4,4,256]{4,0,3,2,1:T(8,128)(2,1)S(1)}, u32[]{:S(2)}, u32[]{:S(2)}) collective-permute-start(bf16[128,1,4,4,256]{4,0,3,2,1:T(8,128)(2,1)S(1)} %get-tuple-element.34), channel_id=1, source_target_pairs={{0,1},{1,2},{2,3},{3,4},{4,5},{5,6},{6,7},{7,8},{8,9},{9,10},{10,1... | collective-permute-start | bytes 3145736 | tf_op jit(solution)/shard_map/ppermute | solution.py:14
  55.8 18.1 %copy-start.2 = (bf16[3,3,3,4,512]{4,3,2,1,0:T(4,128)(2,1)S(1)}, bf16[3,3,3,4,512]{4,3,2,1,0:T(4,128)(2,1)}, u32[]{:S(2)}) copy-start(bf16[3,3,3,4,512]{4,3,2,1,0:T(4,128)(2,1)} %param.6) | copy-start | bytes 331780
  63.0 32.5 %all-to-all-start = ((bf16[256,1,4,256]{3,2,1,0:T(4,128)(2,1)}), bf16[256,1,4,256]{3,2,1,0:T(4,128)(2,1)S(1)}, u32[]{:S(2)}, u32[]{:S(2)}) async-start(bf16[256,1,4,256]{3,2,1,0:T(4,128)(2,1)} %copy.105), calls=%async_computation | async-start | bytes 1048576 | tf_op jit(solution)/shard_map/all_to_all | solution.py:113
  140.6 23.8 %all-to-all-start.1 = ((bf16[4,64,4,256]{3,0,2,1:T(4,128)(2,1)}), bf16[4,64,4,256]{3,0,2,1:T(4,128)(2,1)S(1)}, u32[]{:S(2)}, u32[]{:S(2)}) async-start(bf16[4,64,4,256]{3,0,2,1:T(4,128)(2,1)} %bitcast.260), calls=%async_computation.1 | async-start | bytes 1048576 | tf_op jit(solution)/shard_map/all_to_all | solution.py:134
  147.7 61.7 %all-reduce.93.cloned.1.call-start = ((), (), s32[]{:S(2)}) async-start(), calls=%async_computation.2 | async-start | bytes 442368 | tf_op jit(solution)/shard_map/psum | solution.py:124
  152.5 58.5 %copy-start.1 = (bf16[3,3,3,128,256]{4,3,2,1,0:T(8,128)(2,1)S(1)}, bf16[3,3,3,128,256]{4,3,2,1,0:T(8,128)(2,1)}, u32[]{:S(2)}) copy-start(bf16[3,3,3,128,256]{4,3,2,1,0:T(8,128)(2,1)} %param.5) | copy-start | bytes 5308420
Sparse Core Ops, SparseCore 0:
  10.8 93.5 all-gather.2
  161.5 47.8 all-reduce.92
where the time goes:
time: 219 us; the launch traced here: 218 us
  waiting for transfers between devices  82.9 us (38%)
  local copies, waits for them, and re-layouts  70.2 us (32%)
  starting transfers between devices  20.1 us (9%)
  matrix products  18 us (8%)
  between operations  14.9 us (7%)
  other arithmetic  11.8 us (5%)
    psum x1, waiting for transfers between devices, per_device(): grad_second = lax.psum(weight_grad, 'dp').reshape(3, 3, 3, own_channels, C3)  42.7 us
    unnamed x29, local copies, waits for them, and re-layouts  34.1 us
    all_to_all x1, waiting for transfers between devices, per_device(): lax.all_to_all(hidden, 'space', split_axis=0, concat_axis=1, tiled=True)  20 us
    ppermute x1, waiting for transfers between devices, from_behind(): return lax.ppermute(block, axis, route)  16.5 us
    reshape x1, local copies, waits for them, and re-layouts, per_device(): stacked = jnp.stack(collected, 0).reshape(27 * channels, -1)  16.2 us
    all_to_all x1, starting transfers between devices, per_device(): lax.all_to_all(hidden, 'space', split_axis=0, concat_axis=1, tiled=True)  10.7 us
    unnamed x35, other arithmetic  7.14 us
    dot_general x1, matrix products, contract_last(): lax.dot_general(left_side, right_side, (((1,), (1,)), ((), ())), preferre...  7.13 us
  transfers between devices with their start and end apart: 5, of which 4 were waited for; matrix products, arithmetic and copies ran while one was open for 33% of the time, Pallas kernels for 0%

commit v1 on v0

--- a/solution.py
+++ b/solution.py
@@ -121,7 +121,9 @@
     cot_flat = gathered.reshape(C3, out_cells)
     weight_grad = contract_last(hidden_taps, cot_flat)
     tap_terms = jnp.dot(w_rows, cot_flat, preferred_element_type=jnp.float32)
-    grad_second = lax.psum(weight_grad, "dp").reshape(3, 3, 3, own_channels, C3)
+    grad_second = jnp.sum(lax.all_gather(weight_grad, "dp"), axis=0).reshape(
+        3, 3, 3, own_channels, C3
+    )
 
     def spread(field):
         return jnp.stack(all_taps(field, row_len), 0).reshape(27 * own_channels, -1)

time: 219 us -> 190 us (0.87)
  waiting for transfers between devices: 82.9 us -> 34.5 us
  blocking collectives: 0 us -> 15.3 us
  local copies, waits for them, and re-layouts: 70.2 us -> 73.8 us
    psum x1 -> x0, waiting for transfers between devices: 42.7 us -> none  [per_device(): grad_second = lax.psum(weight_grad, 'dp').reshape(3, 3, 3, own_channels, C3)]
    all_gather x0 -> x1, blocking collectives: none -> 15.3 us  [per_device(): lax.all_gather(weight_grad, 'dp')]
    all_to_all x1, waiting for transfers between devices: 2.99 us -> 0.01 us  [per_device(): lax.all_to_all(back_terms, 'space', split_axis=1, concat_axis=0, tiled=True)]
    another operation x11, local copies, waits for them, and re-layouts: 1.12 us -> 3.62 us  [plane_taps(): rows_out.append(jnp.stack(cols_out, -2))]
    ppermute x1, waiting for transfers between devices: 16.5 us -> 14.3 us  [from_behind(): return lax.ppermute(block, axis, route)]
    unnamed x29 -> x28, local copies, waits for them, and re-layouts: 34.1 us -> 32.5 us
  transfers between devices with their start and end apart: 5 -> 4, of which waited for: 4 -> 2; matrix products, arithmetic and copies ran while one was open for 33% -> 38% of each run, Pallas kernels for 0% -> 0%
where the time goes in v1:
time: 190 us; the launch traced here: 188 us
  local copies, waits for them, and re-layouts  73.8 us (39%)
  waiting for transfers between devices  34.5 us (18%)
  starting transfers between devices  18.8 us (10%)
  matrix products  17.2 us (9%)
  blocking collectives  15.3 us (8%)
  between operations  14.9 us (8%)
  other arithmetic  13.6 us (7%)
    unnamed x28, local copies, waits for them, and re-layouts  32.5 us
    all_to_all x1, waiting for transfers between devices, per_device(): lax.all_to_all(hidden, 'space', split_axis=0, concat_axis=1, tiled=True)  20.2 us
    reshape x1, local copies, waits for them, and re-layouts, per_device(): stacked = jnp.stack(collected, 0).reshape(27 * channels, -1)  16.2 us
    all_gather x1, blocking collectives, per_device(): lax.all_gather(weight_grad, 'dp')  15.3 us
    ppermute x1, waiting for transfers between devices, from_behind(): return lax.ppermute(block, axis, route)  14.3 us
    all_to_all x1, starting transfers between devices, per_device(): lax.all_to_all(hidden, 'space', split_axis=0, concat_axis=1, tiled=True)  10 us
    unnamed x35, other arithmetic  7.03 us
    another operation x1, local copies, waits for them, and re-layouts, per_device(): stacked = jnp.stack(collected, 0).reshape(27 * channels, -1)  6.8 us
  transfers between devices with their start and end apart: 4, of which 2 were waited for; matrix products, arithmetic and copies ran while one was open for 38% of the time, Pallas kernels for 0%

profile of v1, /device:TPU:8, one launch (start us, length us, event | category | flops | bytes accessed | tf_op | source)
XLA Modules:
  0.0 188.1 jit_solution(14873679694465059724)
XLA Ops:
  7.2 2.9 %copy.103 = bf16[1,128,2,16,256]{4,1,3,2,0:T(8,128)(2,1)S(1)} copy(bf16[1,128,2,16,256]{4,3,2,1,0:T(8,128)(2,1)} %param.4) | data formatting | bytes 4194304 | tf_op args[0]
  10.1 1.1 slice_bitcast_fusion
  11.2 1.9 %collective-permute-start = (bf16[128,1,4,4,256]{4,0,3,2,1:T(8,128)(2,1)S(1)}, bf16[128,1,4,4,256]{4,0,3,2,1:T(8,128)(2,1)}, u32[]{:S(2)}, u32[]{:S(2)}) collective-permute-start(bf16[128,1,4,4,256]{4,0,3,2,1:T(8,128)(2,1)S(1)} %get-tuple-element.34), channel_id=1, source_target_pairs={{0,1},{1,2},{2,3},{3,4},{4,5},{5,6},{6,7},{7,8},{8,9},{9,10},{10,1... | collective-permute-start | bytes 3145736 | tf_op jit(solution)/shard_map/ppermute | solution.py:14
  13.1 1.0 slice_bitcast_fusion.45
  14.7 1.4 slice_bitcast_fusion.58
  16.6 14.3 %collective-permute-done = bf16[128,1,4,4,256]{4,0,3,2,1:T(8,128)(2,1)} collective-permute-done((bf16[128,1,4,4,256]{4,0,3,2,1:T(8,128)(2,1)S(1)}, bf16[128,1,4,4,256]{4,0,3,2,1:T(8,128)(2,1)}, u32[]{:S(2)}, u32[]{:S(2)}) %collective-permute-start) | collective-permute-done | bytes 1048608 | tf_op jit(solution)/shard_map/ppermute | solution.py:14
  30.9 1.0 slice_bitcast_fusion.73
  32.0 1.4 slice_bitcast_fusion.72
  35.3 6.8 %copy.104 = bf16[27,128,1,2,2,256]{5,4,3,1,0,2:T(2,128)(2,1)} copy(bf16[27,128,1,2,2,256]{5,1,4,3,2,0:T(8,128)(2,1)S(1)} %fusion.33) | data formatting | bytes 14155776 | tf_op jit(solution)/shard_map/stack | solution.py:110
  42.1 16.2 %reshape.233 = bf16[3456,1024]{1,0:T(8,128)(2,1)} reshape(bf16[27,128,1,2,2,256]{5,4,3,1,0,2:T(2,128)(2,1)} %copy.104) | data formatting | bytes 14155776 | tf_op jit(solution)/shard_map/reshape | solution.py:110
  58.3 6.2 %fusion.2 = (bf16[256,1024]{0,1:T(8,128)(2,1)S(1)}, f32[1024,256]{1,0:T(8,128)}) fusion(bf16[3456,1024]{1,0:T(8,128)(2,1)} %reshape.233, bf16[3456,256]{1,0:T(8,128)(2,1)S(1)} %bitcast.643), kind=kOutput, calls=%fused_computation.10 | convolution fusion | flops 1814036480 | bytes 10420224 | tf_op jit(solution)/shard_map/dot_general | solution.py:83
  64.4 1.1 copy.105
  65.5 10.0 %all-to-all-start = ((bf16[256,1,4,256]{3,2,1,0:T(4,128)(2,1)}), bf16[256,1,4,256]{3,2,1,0:T(4,128)(2,1)S(1)}, u32[]{:S(2)}, u32[]{:S(2)}) async-start(bf16[256,1,4,256]{3,2,1,0:T(4,128)(2,1)} %copy.105), calls=%async_computation | async-start | bytes 1048576 | tf_op jit(solution)/shard_map/all_to_all | solution.py:113
  75.6 1.6 copy.142
  77.3 20.2 %all-to-all-done = bf16[256,1,4,256]{3,2,1,0:T(4,128)(2,1)S(1)} async-done(((bf16[256,1,4,256]{3,2,1,0:T(4,128)(2,1)}), bf16[256,1,4,256]{3,2,1,0:T(4,128)(2,1)S(1)}, u32[]{:S(2)}, u32[]{:S(2)}) %all-to-all-start) | async-done | bytes 524320 | tf_op jit(solution)/shard_map/all_to_all | solution.py:113
  98.3 0.7 constant_dynamic-update-slice_fusion.26
  99.0 0.7 constant_dynamic-update-slice_fusion.25
  99.8 0.7 constant_dynamic-update-slice_fusion.24
  100.5 0.7 constant_dynamic-update-slice_fusion.23
  101.2 0.6 constant_dynamic-update-slice_fusion.22
  101.9 0.6 constant_dynamic-update-slice_fusion.21
  102.5 0.7 constant_dynamic-update-slice_fusion.20
  103.2 0.6 constant_dynamic-update-slice_fusion.19
  103.9 0.6 constant_dynamic-update-slice_fusion.18
  104.7 0.7 constant_dynamic-update-slice_fusion.17
  105.4 0.7 constant_dynamic-update-slice_fusion.16
  106.2 0.7 constant_dynamic-update-slice_fusion.15
  107.1 0.7 constant_dynamic-update-slice_fusion.14
  108.4 0.6 constant_dynamic-update-slice_fusion.12
  109.1 0.7 constant_dynamic-update-slice_fusion.11
  111.1 0.7 constant_dynamic-update-slice_fusion.8
  111.8 0.7 constant_dynamic-update-slice_fusion.7
  112.5 0.7 constant_dynamic-update-slice_fusion.6
  113.3 0.7 constant_dynamic-update-slice_fusion.5
  114.6 0.6 constant_dynamic-update-slice_fusion.3
  115.3 0.7 constant_dynamic-update-slice_fusion.2
  116.6 16.7 %copy.149 = bf16[64,8,32,256]{3,1,2,0:T(8,128)(2,1)} copy(bf16[64,8,32,256]{3,2,1,0:T(8,128)(2,1)} %bitcast.646) | data formatting | bytes 16777216
  133.3 4.7 %fusion.41 = f32[108,8192]{1,0:T(8,128)S(1)} fusion(bf16[108,512]{1,0:T(8,128)(2,1)S(1)} %reshape.238, bf16[512,8192]{1,0:T(8,128)(2,1)} %bitcast.644), kind=kOutput, calls=%fused_computation.302 | convolution fusion | flops 905969664 | bytes 12038144 | tf_op jit(solution)/shard_map/dot_general | solution.py:123
  138.7 0.7 slice_select_fusion.8
  141.9 1.1 copy.140
  143.0 6.8 %all-to-all-start.1 = ((bf16[4,64,4,256]{3,0,2,1:T(4,128)(2,1)}), bf16[4,64,4,256]{3,0,2,1:T(4,128)(2,1)S(1)}, u32[]{:S(2)}, u32[]{:S(2)}) async-start(bf16[4,64,4,256]{3,0,2,1:T(4,128)(2,1)} %bitcast.261), calls=%async_computation.1 | async-start | bytes 1048576 | tf_op jit(solution)/shard_map/all_to_all | solution.py:136
  150.4 1.8 copy.111
  152.4 1.2 copy.150
  153.6 6.3 %convolution_bitcast_fusion = f32[1,108,512]{2,1,0:T(8,128)S(1)} fusion(bf16[108,8192]{1,0:T(8,128)(2,1)S(1)} %bitcast.648, bf16[512,8192]{1,0:T(8,128)(2,1)} %bitcast.645), kind=kOutput, calls=%fused_computation | convolution fusion | flops 905969664 | bytes 10379264 | tf_op jit(solution)/shard_map/dot_general | solution.py:89
  160.0 15.3 %all-gather.2 = f32[4,108,512]{2,1,0:T(8,128)} all-gather(f32[1,108,512]{2,1,0:T(8,128)S(1)} %convolution_bitcast_fusion), channel_id=3, replica_groups=mesh['dp'=4,'space'=64] {'dp'}, dimensions={0}, use_global_device_ids=true | all-gather | bytes 1105920 | tf_op jit(solution)/shard_map/all_gather | solution.py:124
  175.3 2.0 %reduce_sum.9 = f32[108,512]{1,0:T(8,128)} reduce(f32[4,108,512]{2,1,0:T(8,128)} %all-gather.2, f32[]{:T(128)} %constant.147.clone.1), dimensions={0}, to_apply=%region_0.1 | reduce | flops 165888 | bytes 1105924 | tf_op jit(solution)/shard_map/reduce_sum | solution.py:124
  177.2 1.7 reshape.237
  179.5 1.8 fusion
  (120 shorter events, 11.6 us)
Async XLA Ops:
  7.2 51.1 %copy-start = (bf16[3,3,3,128,256]{4,3,2,1,0:T(8,128)(2,1)S(1)}, bf16[3,3,3,128,256]{4,3,2,1,0:T(8,128)(2,1)}, u32[]{:S(2)}) copy-start(bf16[3,3,3,128,256]{4,3,2,1,0:T(8,128)(2,1)} %param.5) | copy-start | bytes 5308420
  7.2 109.4 %all-gather.5.cloned.1.call-start = ((), (), s32[]{:S(2)}) async-start(), calls=%async_computation.2 | async-start | bytes 8519680 | tf_op jit(solution)/shard_map/all_gather | solution.py:120
  11.2 19.7 %collective-permute-start = (bf16[128,1,4,4,256]{4,0,3,2,1:T(8,128)(2,1)S(1)}, bf16[128,1,4,4,256]{4,0,3,2,1:T(8,128)(2,1)}, u32[]{:S(2)}, u32[]{:S(2)}) collective-permute-start(bf16[128,1,4,4,256]{4,0,3,2,1:T(8,128)(2,1)S(1)} %get-tuple-element.34), channel_id=1, source_target_pairs={{0,1},{1,2},{2,3},{3,4},{4,5},{5,6},{6,7},{7,8},{8,9},{9,10},{10,1... | collective-permute-start | bytes 3145736 | tf_op jit(solution)/shard_map/ppermute | solution.py:14
  58.3 17.3 %copy-start.2 = (bf16[3,3,3,4,512]{4,3,2,1,0:T(4,128)(2,1)S(1)}, bf16[3,3,3,4,512]{4,3,2,1,0:T(4,128)(2,1)}, u32[]{:S(2)}) copy-start(bf16[3,3,3,4,512]{4,3,2,1,0:T(4,128)(2,1)} %param.6) | copy-start | bytes 331780
  65.5 32.0 %all-to-all-start = ((bf16[256,1,4,256]{3,2,1,0:T(4,128)(2,1)}), bf16[256,1,4,256]{3,2,1,0:T(4,128)(2,1)S(1)}, u32[]{:S(2)}, u32[]{:S(2)}) async-start(bf16[256,1,4,256]{3,2,1,0:T(4,128)(2,1)} %copy.105), calls=%async_computation | async-start | bytes 1048576 | tf_op jit(solution)/shard_map/all_to_all | solution.py:113
  143.0 35.9 %all-to-all-start.1 = ((bf16[4,64,4,256]{3,0,2,1:T(4,128)(2,1)}), bf16[4,64,4,256]{3,0,2,1:T(4,128)(2,1)S(1)}, u32[]{:S(2)}, u32[]{:S(2)}) async-start(bf16[4,64,4,256]{3,0,2,1:T(4,128)(2,1)} %bitcast.261), calls=%async_computation.1 | async-start | bytes 1048576 | tf_op jit(solution)/shard_map/all_to_all | solution.py:136
  160.0 21.3 %copy-start.1 = (bf16[3,3,3,128,256]{4,3,2,1,0:T(8,128)(2,1)S(1)}, bf16[3,3,3,128,256]{4,3,2,1,0:T(8,128)(2,1)}, u32[]{:S(2)}) copy-start(bf16[3,3,3,128,256]{4,3,2,1,0:T(8,128)(2,1)} %param.5) | copy-start | bytes 5308420
Sparse Core Ops, SparseCore 0:
  13.3 95.7 all-gather.4
